TPU v7x, 32 devices: a whole 2x2x4 slice. The times are simulated.
32 devices in a mesh: expert: 4 (over y, x), tensor: 2 (over core), dp: 4 (over z).
Axes of the slice: x: 2, y: 2, z: 4, core: 2. Of those that a mesh axis runs over, the one named last changes fastest.
Arguments:
- tokens: bfloat16 [2048, 3072], P(('expert', 'dp'), 'tensor'), may hold values from -6 to 6
- experts_chosen: int32 [2048, 2], P(('expert', 'dp')), may hold values from 0 to 3, all different within a row; in each aligned block of 128 rows (0 to 127, 128 to 255, ...) at most 73 rows name the same one
- route_weights: float32 [2048, 2], P(('expert', 'dp')), may hold values from 0.1 to 1
- cotangent: bfloat16 [2048, 3072], P(('expert', 'dp'), 'tensor'), may hold values from -6 to 6
- gate_weight: bfloat16 [4, 3072, 8192], P('expert', 'dp', 'tensor'), may hold values from -0.15625 to 0.15625
- up_weight: bfloat16 [4, 3072, 8192], P('expert', 'dp', 'tensor'), may hold values from -0.15625 to 0.15625
- down_weight: bfloat16 [4, 8192, 3072], P('expert', 'tensor', 'dp'), may hold values from -0.09375 to 0.09375
Outputs:
- layer_output: bfloat16 [2048, 3072], P(('expert', 'dp'), 'tensor')
- token_grad: bfloat16 [2048, 3072], P(('expert', 'dp'), 'tensor')
- route_grad: float32 [2048, 2], P(('expert', 'dp'))
Inputs may be any that keep to these rules, and one draw needn't show every extreme that they name: `experts_chosen`: each row names 2 different experts. Among the 128 rows of one index of expert+dp no expert is named more than 73 times, and in some such block one expert is named exactly 73 times.
All inputs are finite; a program needn't handle non-finite values.
Results may differ from a plain program's by a relative error of at most 0.0072.
Values may be sent and summed in bfloat16 or wider, within the bound.
No kernel may reach another device: no remote copies, remote signals or barrier semaphores. Data moves between devices by JAX's collectives and lax.ppermute only.
A program may use at most 256 MiB of HBM per device.

v0:
```python
import jax
import jax.numpy as jnp
from jax import lax
from jax.sharding import PartitionSpec as P


def slot_table(experts_chosen, num_experts, cap_rows):
    flat_ids = experts_chosen.reshape(-1)
    expert_hot = (flat_ids[:, None] == jnp.arange(num_experts, dtype=jnp.int32)[None, :]).astype(
        jnp.int32
    )
    earlier = jnp.cumsum(expert_hot, axis=0) - expert_hot
    rank_slot = jnp.sum(earlier * expert_hot, axis=1)
    target = flat_ids * cap_rows + rank_slot
    all_slots = jnp.arange(num_experts * cap_rows, dtype=jnp.int32)
    return (target[:, None] == all_slots[None, :]).astype(jnp.bfloat16)


def to_slots(slot_onehot, pair_rows, num_experts, cap_rows):
    packed = jnp.einsum("ps,pd->sd", slot_onehot, pair_rows, preferred_element_type=jnp.float32)
    return packed.astype(jnp.bfloat16).reshape(num_experts, cap_rows, pair_rows.shape[1])


def from_slots(slot_onehot, returned):
    flat_back = returned.reshape(-1, returned.shape[2])
    return jnp.dot(slot_onehot, flat_back, preferred_element_type=jnp.float32)


def as_blocks(summed, num_experts, cap_rows):
    return summed.astype(jnp.bfloat16).reshape(num_experts, cap_rows, summed.shape[1])


def local(tokens, experts_chosen, route_weights, cotangent, gate_weight, up_weight, down_weight):
    tok_rows, feat_cols = tokens.shape
    top_count = experts_chosen.shape[1]
    num_experts = lax.axis_size("expert")
    cap_rows = min(tok_rows, 9 * tok_rows * top_count // (8 * num_experts) + 1)
    slot_onehot = slot_table(experts_chosen, num_experts, cap_rows)
    pair_weights = route_weights.reshape(-1, 1)
    token_pairs = jnp.repeat(tokens, top_count, axis=0)
    grad_pairs = (
        jnp.repeat(cotangent, top_count, axis=0).astype(jnp.float32) * pair_weights
    ).astype(jnp.bfloat16)
    token_send = to_slots(slot_onehot, token_pairs, num_experts, cap_rows)
    grad_send = to_slots(slot_onehot, grad_pairs, num_experts, cap_rows)
    token_recv = lax.all_to_all(token_send, "expert", split_axis=0, concat_axis=0, tiled=True)
    token_full = lax.all_gather(token_recv, "tensor", axis=2, tiled=True)
    model_cols = token_full.shape[2]
    token_rows = token_full.reshape(-1, model_cols)
    gate_all, up_all = (
        lax.all_gather(gate_weight, "dp", axis=1, tiled=True),
        lax.all_gather(up_weight, "dp", axis=1, tiled=True),
    )
    gate_pre = jnp.dot(token_rows, gate_all[0], preferred_element_type=jnp.float32)
    up_pre = jnp.dot(token_rows, up_all[0], preferred_element_type=jnp.float32)
    hidden = (jax.nn.silu(gate_pre) * up_pre).astype(jnp.bfloat16)
    down_all = lax.all_gather(down_weight, "dp", axis=2, tiled=True)
    out_part = jnp.dot(hidden, down_all[0], preferred_element_type=jnp.float32)
    out_sum = lax.psum_scatter(
        out_part.astype(jnp.bfloat16), "tensor", scatter_dimension=1, tiled=True
    ).astype(jnp.float32)
    out_back = lax.all_to_all(
        as_blocks(out_sum, num_experts, cap_rows), "expert", split_axis=0, concat_axis=0, tiled=True
    )
    grad_recv = lax.all_to_all(grad_send, "expert", split_axis=0, concat_axis=0, tiled=True)
    grad_full = lax.all_gather(grad_recv, "tensor", axis=2, tiled=True)
    grad_rows_all = grad_full.reshape(-1, model_cols)
    contract = (((1,), (1,)), ((), ()))
    hidden_grad = lax.dot_general(
        grad_rows_all, down_all[0], contract, preferred_element_type=jnp.float32
    )
    sigmoid_gate = jax.nn.sigmoid(gate_pre)
    up_grad = (hidden_grad * jax.nn.silu(gate_pre)).astype(jnp.bfloat16)
    gate_grad = (
        hidden_grad * up_pre * sigmoid_gate * (1.0 + gate_pre * (1.0 - sigmoid_gate))
    ).astype(jnp.bfloat16)
    in_part = lax.dot_general(gate_grad, gate_all[0], contract, preferred_element_type=jnp.float32)
    in_part = in_part + lax.dot_general(
        up_grad, up_all[0], contract, preferred_element_type=jnp.float32
    )
    in_sum = lax.psum_scatter(
        in_part.astype(jnp.bfloat16), "tensor", scatter_dimension=1, tiled=True
    ).astype(jnp.float32)
    in_back = lax.all_to_all(
        as_blocks(in_sum, num_experts, cap_rows), "expert", split_axis=0, concat_axis=0, tiled=True
    )
    out_pairs = from_slots(slot_onehot, out_back).reshape(tok_rows, top_count, feat_cols)
    in_pairs = from_slots(slot_onehot, in_back).reshape(tok_rows, top_count, feat_cols)
    layer_output = jnp.sum(route_weights[:, :, None] * out_pairs, axis=1).astype(jnp.bfloat16)
    token_grad = jnp.sum(in_pairs, axis=1).astype(jnp.bfloat16)
    local_dots = jnp.sum(cotangent.astype(jnp.float32)[:, None, :] * out_pairs, axis=2)
    route_grad = lax.psum(local_dots, "tensor")
    return (layer_output, token_grad, route_grad)


def solution(mesh):
    in_specs = (
        P(("expert", "dp"), "tensor"),
        P(("expert", "dp"), None),
        P(("expert", "dp"), None),
        P(("expert", "dp"), "tensor"),
        P("expert", "dp", "tensor"),
        P("expert", "dp", "tensor"),
        P("expert", "tensor", "dp"),
    )
    out_specs = (
        P(("expert", "dp"), "tensor"),
        P(("expert", "dp"), "tensor"),
        P(("expert", "dp"), None),
    )
    return jax.shard_map(local, mesh=mesh, in_specs=in_specs, out_specs=out_specs, check_vma=False)
```

profile of v0, /device:TPU:0, one launch (start us, length us, event | category | flops | bytes accessed | tf_op | source)
XLA Modules:
  0.0 1455.3 jit_solution(10602917999644850191)
XLA Ops:
  7.2 0.8 copy.21
  8.3 1.4 broadcast_in_dim.4
  10.1 1.2 reduce-window.6
  12.5 18.7 %all_to_all.20 = bf16[4,73,1536]{2,1,0:T(8,128)(2,1)} all-to-all(bf16[4,73,1536]{2,1,0:T(8,128)(2,1)S(1)} %reshape.107), channel_id=1, replica_groups=mesh['expert'=4,'tensor'=2,'dp'=4] {'expert'}, dimensions={0} | all-to-all | bytes 1794048 | tf_op jit(solution)/shard_map/all_to_all | solution.py:46
  31.7 1.1 convert_element_type.57
  33.0 0.5 convolution_convert_fusion
  33.8 15.7 %all_to_all.21 = bf16[4,73,1536]{2,1,0:T(8,128)(2,1)} all-to-all(bf16[4,73,1536]{2,1,0:T(8,128)(2,1)S(1)} %reshape.111), channel_id=1, replica_groups=mesh['expert'=4,'tensor'=2,'dp'=4] {'expert'}, dimensions={0} | all-to-all | bytes 1794048 | tf_op jit(solution)/shard_map/all_to_all | solution.py:65
  49.6 0.7 all-gather.10.cloned.1.call-update
  50.9 0.5 all-gather.12.cloned.1.call-update
  51.7 2.0 reshape.108
  53.7 5.9 all-gather.14.cloned.1.call-done
  59.6 3.3 reshape.112
  62.9 424.7 %all-gather.10.cloned.1.call-done = bf16[1,3072,4096]{2,1,0:T(8,128)(2,1)} async-done(((bf16[1,768,4096]{2,1,0:T(8,128)(2,1)}), bf16[1,3072,4096]{2,1,0:T(8,128)(2,1)}) %all-gather.10.cloned.1.call-update) | async-done | bytes 25165840 | tf_op jit(solution)/shard_map/all_gather | solution.py:52
  487.6 16.4 %fusion.6 = f32[292,4096]{1,0:T(8,128)} fusion(bf16[292,3072]{1,0:T(8,128)(2,1)S(1)} %reshape.108, bf16[1,3072,4096]{2,1,0:T(8,128)(2,1)} %all-gather.10.cloned.1.call-done), kind=kOutput, calls=%fused_computation.6 | convolution fusion | flops 7348420608 | bytes 31744000 | tf_op jit(solution)/shard_map/dot_general | solution.py:55
  504.0 408.4 %all-gather.8.cloned.1.call-done = bf16[1,3072,4096]{2,1,0:T(8,128)(2,1)} async-done(((bf16[1,768,4096]{2,1,0:T(8,128)(2,1)}), bf16[1,3072,4096]{2,1,0:T(8,128)(2,1)}) %all-gather.8.cloned.1.call-update) | async-done | bytes 25165840 | tf_op jit(solution)/shard_map/all_gather | solution.py:51
  912.4 16.3 %fusion.10 = f32[292,4096]{1,0:T(8,128)} fusion(bf16[292,3072]{1,0:T(8,128)(2,1)S(1)} %reshape.108, bf16[1,3072,4096]{2,1,0:T(8,128)(2,1)} %all-gather.8.cloned.1.call-done), kind=kOutput, calls=%fused_computation.10 | convolution fusion | flops 7348420608 | bytes 31744000 | tf_op jit(solution)/shard_map/dot_general | solution.py:54
  928.8 408.5 %all-gather.12.cloned.1.call-done = bf16[1,4096,3072]{2,1,0:T(8,128)(2,1)} async-done(((bf16[1,4096,768]{2,1,0:T(8,128)(2,1)}), bf16[1,4096,3072]{2,1,0:T(8,128)(2,1)}) %all-gather.12.cloned.1.call-update) | async-done | bytes 25165840 | tf_op jit(solution)/shard_map/all_gather | solution.py:57
  1337.3 14.5 fusion
  1351.7 16.7 %fusion.4 = f32[292,3072]{1,0:T(8,128)} fusion(bf16[1,3072,4096]{2,1,0:T(8,128)(2,1)} %all-gather.10.cloned.1.call-done, f32[292,4096]{1,0:T(8,128)} %fusion, f32[292,4096]{1,0:T(8,128)} %fusion.10), kind=kOutput, calls=%fused_computation.4 | convolution fusion | flops 7355596800 | bytes 38322176 | tf_op jit(solution)/shard_map/dot_general | solution.py:78
  1368.5 21.3 %fusion.16 = bf16[292,3072]{1,0:T(8,128)(2,1)} fusion(f32[292,3072]{1,0:T(8,128)} %fusion.4, bf16[1,3072,4096]{2,1,0:T(8,128)(2,1)} %all-gather.8.cloned.1.call-done, f32[292,4096]{1,0:T(8,128)} %fusion.10, f32[292,4096]{1,0:T(8,128)} %fusion, f32[292,4096]{1,0:T(8,128)} %fusion.6), kind=kOutput, calls=%fused_computation.18 | convolution fusion | flops 7362174976 | bytes 44900352 | tf_op jit(solution)/shard_map/dot_general | solution.py:77
  1389.9 17.2 %fusion.19 = bf16[292,3072]{1,0:T(8,128)(2,1)} fusion(bf16[1,4096,3072]{2,1,0:T(8,128)(2,1)} %all-gather.12.cloned.1.call-done, f32[292,4096]{1,0:T(8,128)} %fusion.6, f32[292,4096]{1,0:T(8,128)} %fusion.10), kind=kOutput, calls=%fused_computation.19 | convolution fusion | flops 7356493824 | bytes 36528128 | tf_op jit(solution)/shard_map/dot_general | solution.py:58
  1407.1 2.4 reshape.113
  1409.5 3.6 all-to-all-start.3
  1413.2 1.5 reduce-scatter.3.cloned.1.call-done
  1414.7 2.4 reshape.109
  1417.1 9.3 all-to-all-done.3
  1426.5 3.5 all-to-all-start.1
  1430.0 1.0 convert_element_type.56
  1431.5 1.4 convolution_reduce_fusion
  1432.8 9.6 all-to-all-done.1
  1442.7 2.7 multiply_reduce_fusion
  1445.4 3.0 psum.7
  (43 shorter events, 4.5 us)
Async XLA Ops:
  7.2 24.1 %copy-start = (bf16[128,1536]{1,0:T(8,128)(2,1)S(1)}, bf16[128,1536]{1,0:T(8,128)(2,1)}, u32[]{:S(2)}) copy-start(bf16[128,1536]{1,0:T(8,128)(2,1)} %param.10) | copy-start | bytes 1179652
  7.2 44.5 %all-gather.6.cloned.1.call-start = ((), (), s32[]{:S(2)}) async-start(), calls=%async_computation.6 | async-start | bytes 2949120 | tf_op jit(solution)/shard_map/all_gather | solution.py:47
  12.2 20.5 %copy-start.2 = (f32[128,2]{0,1:T(2,128)S(1)}, f32[128,2]{0,1:T(2,128)}, u32[]{:S(2)}) copy-start(f32[128,2]{0,1:T(2,128)} %param.9) | copy-start | bytes 3076
  31.2 28.4 %all-gather.14.cloned.1.call-start = ((), (), s32[]{:S(2)}) async-start(), calls=%async_computation.11 | async-start | bytes 2949120 | tf_op jit(solution)/shard_map/all_gather | solution.py:66
  49.5 438.1 %all-gather.10.cloned.1.call-start = ((), (), s32[]{:S(2)}) async-start(), calls=%async_computation.8 | async-start | bytes 31457280 | tf_op jit(solution)/shard_map/all_gather | solution.py:52
  50.3 862.2 %all-gather.8.cloned.1.call-start = ((), (), s32[]{:S(2)}) async-start(), calls=%async_computation.7 | async-start | bytes 31457280 | tf_op jit(solution)/shard_map/all_gather | solution.py:51
  50.9 1286.4 %all-gather.12.cloned.1.call-start = ((), (), s32[]{:S(2)}) async-start(), calls=%async_computation.9 | async-start | bytes 31457280 | tf_op jit(solution)/shard_map/all_gather | solution.py:57
  51.5 1355.7 %reduce-scatter.5.cloned.1.call-start = ((), (), s32[]{:S(2)}) async-start(), calls=%async_computation.12 | async-start | bytes 2727936 | tf_op jit(solution)/shard_map/reduce_scatter | solution.py:81
  1389.8 24.9 %reduce-scatter.3.cloned.1.call-start = ((), (), s32[]{:S(2)}) async-start(), calls=%async_computation.10 | async-start | bytes 2727936 | tf_op jit(solution)/shard_map/reduce_scatter | solution.py:59
  1407.1 24.1 %copy-start.1 = (s32[128,2]{0,1:T(2,128)S(1)}, s32[128,2]{0,1:T(2,128)}, u32[]{:S(2)}) copy-start(s32[128,2]{0,1:T(2,128)} %param.8) | copy-start | bytes 3076
  1409.5 16.9 %all-to-all-start.3 = ((bf16[4,73,1536]{2,1,0:T(8,128)(2,1)}), bf16[4,73,1536]{2,1,0:T(8,128)(2,1)S(1)}, u32[]{:S(2)}, u32[]{:S(2)}) async-start(bf16[4,73,1536]{2,1,0:T(8,128)(2,1)} %reshape.113), calls=%async_computation.5 | async-start | bytes 1966080 | tf_op jit(solution)/shard_map/all_to_all | solution.py:84
  1426.5 16.0 %all-to-all-start.1 = ((bf16[4,73,1536]{2,1,0:T(8,128)(2,1)}), bf16[4,73,1536]{2,1,0:T(8,128)(2,1)S(1)}, u32[]{:S(2)}, u32[]{:S(2)}) async-start(bf16[4,73,1536]{2,1,0:T(8,128)(2,1)} %reshape.109), calls=%async_computation.2 | async-start | bytes 1966080 | tf_op jit(solution)/shard_map/all_to_all | solution.py:62
Sparse Core Ops, SparseCore 0:
  31.3 9.9 all-gather.5
  49.7 9.9 all-gather.13
  61.2 426.3 all-gather.9
  489.0 423.3 all-gather.7
  913.9 423.3 all-gather.11
  1389.9 7.5 reduce-scatter.4
  1407.2 7.4 reduce-scatter.2
where the time goes:
time: 1460 us
  waiting for transfers between devices  1270 us (87%)
  matrix products  108 us (7%)
  blocking collectives  37.4 us (3%)
  local copies, waits for them, and re-layouts  16.2 us (1%)
    all_gather x1, waiting for transfers between devices, local(): lax.all_gather(up_weight, 'dp', axis=1, tiled=True)  425 us
    all_gather x1, waiting for transfers between devices, local(): down_all = lax.all_gather(down_weight, 'dp', axis=2, tiled=True)  408 us
    all_gather x1, waiting for transfers between devices, local(): lax.all_gather(gate_weight, 'dp', axis=1, tiled=True)  408 us
  transfers between devices with their start and end apart: 9, of which 7 were waited for; matrix products, arithmetic and copies ran while one was open for 4% of the time, Pallas kernels for 0%

commit v1 on v0

--- a/solution.py
+++ b/solution.py
@@ -2,6 +2,23 @@
 import jax.numpy as jnp
 from jax import lax
 from jax.sharding import PartitionSpec as P
+
+
+def joined_along(blocks, dim):
+    blocks = jnp.moveaxis(blocks, 0, dim)
+    shape = blocks.shape
+    return blocks.reshape(*shape[:dim], shape[dim] * shape[dim + 1], *shape[dim + 2 :])
+
+
+def gather_around(value, axis, dim):
+    size = lax.axis_size(axis)
+    ahead = [(i, (i + 1) % size) for i in range(size)]
+    pieces = [value]
+    while len(pieces) < size:
+        pieces.append(lax.ppermute(pieces[-1], axis, ahead))
+    position = lax.axis_index(axis)
+    pieces = jnp.stack(pieces)[(position - jnp.arange(size)) % size]
+    return joined_along(pieces, dim)
 
 
 def slot_table(experts_chosen, num_experts, cap_rows):
@@ -48,7 +65,7 @@
     model_cols = token_full.shape[2]
     token_rows = token_full.reshape(-1, model_cols)
     gate_all, up_all = (
-        lax.all_gather(gate_weight, "dp", axis=1, tiled=True),
+        gather_around(gate_weight, "dp", 1),
         lax.all_gather(up_weight, "dp", axis=1, tiled=True),
     )
     gate_pre = jnp.dot(token_rows, gate_all[0], preferred_element_type=jnp.float32)

time: 1460 us -> 1390 us (0.952)
  waiting for transfers between devices: 1270 us -> 949 us
  starting transfers between devices: 7.58 us -> 177 us
  local copies, waits for them, and re-layouts: 16.2 us -> 64 us
  other arithmetic: 2.35 us -> 40.8 us
    ppermute x0 -> x3, waiting for transfers between devices: none -> 754 us  [gather_around(): pieces.append(lax.ppermute(pieces[-1], axis, ahead))]
    all_gather x1, waiting for transfers between devices: 425 us -> 0.01 us  [local(): lax.all_gather(up_weight, 'dp', axis=1, tiled=True)]
    all_gather x1 -> x0, waiting for transfers between devices: 408 us -> none  [local(): lax.all_gather(gate_weight, 'dp', axis=1, tiled=True)]
    all_gather x1, waiting for transfers between devices: 408 us -> 173 us  [local(): down_all = lax.all_gather(down_weight, 'dp', axis=2, tiled=True)]
    ppermute x0 -> x3, starting transfers between devices: none -> 169 us  [gather_around(): pieces.append(lax.ppermute(pieces[-1], axis, ahead))]
    gather x0 -> x5, local copies, waits for them, and re-layouts: none -> 44.6 us  [gather_around(): pieces = jnp.stack(pieces)[(position - jnp.arange(size)) % size]]
    another operation x2 -> x3, other arithmetic: 1.26 us -> 22.1 us  [the longest x1 20.8 us: gather_around(): pieces = jnp.stack(pieces)[(position - jnp.arange(size)) % size]]
    unnamed x1 -> x2, other arithmetic: 0.07 us -> 17.7 us
  transfers between devices with their start and end apart: 9 -> 11, of which waited for: 7 -> 7; matrix products, arithmetic and copies ran while one was open for 4% -> 10% of each run, Pallas kernels for 0% -> 0%
where the time goes in v1:
time: 1390 us
  waiting for transfers between devices  949 us (68%)
  starting transfers between devices  177 us (13%)
  matrix products  104 us (7%)
  local copies, waits for them, and re-layouts  64 us (5%)
  other arithmetic  40.8 us (3%)
  blocking collectives  37.3 us (3%)
  between operations  14.3 us (1%)
    ppermute x3, waiting for transfers between devices, gather_around(): pieces.append(lax.ppermute(pieces[-1], axis, ahead))  754 us
    all_gather x1, waiting for transfers between devices, local(): down_all = lax.all_gather(down_weight, 'dp', axis=2, tiled=True)  173 us
    ppermute x3, starting transfers between devices, gather_around(): pieces.append(lax.ppermute(pieces[-1], axis, ahead))  169 us
    gather x5, local copies, waits for them, and re-layouts, gather_around(): pieces = jnp.stack(pieces)[(position - jnp.arange(size)) % size]  44.6 us
  transfers between devices with their start and end apart: 11, of which 7 were waited for; matrix products, arithmetic and copies ran while one was open for 10% of the time, Pallas kernels for 0%

profile of v1, /device:TPU:0, one launch (start us, length us, event | category | flops | bytes accessed | tf_op | source)
XLA Modules:
  0.0 1386.0 jit_solution(8597672696583736749)
XLA Ops:
  13.1 18.7 %all_to_all.20 = bf16[4,73,1536]{2,1,0:T(8,128)(2,1)} all-to-all(bf16[4,73,1536]{2,1,0:T(8,128)(2,1)S(1)} %reshape.156), channel_id=1, replica_groups=mesh['expert'=4,'tensor'=2,'dp'=4] {'expert'}, dimensions={0} | all-to-all | bytes 1794048 | tf_op jit(solution)/shard_map/all_to_all | solution.py:63
  34.4 15.7 %all_to_all.21 = bf16[4,73,1536]{2,1,0:T(8,128)(2,1)} all-to-all(bf16[4,73,1536]{2,1,0:T(8,128)(2,1)S(1)} %reshape.160), channel_id=1, replica_groups=mesh['expert'=4,'tensor'=2,'dp'=4] {'expert'}, dimensions={0} | all-to-all | bytes 1794048 | tf_op jit(solution)/shard_map/all_to_all | solution.py:82
  53.1 244.2 %collective-permute-done = bf16[1,768,4096]{2,1,0:T(8,128)(2,1)S(1)} collective-permute-done((bf16[1,768,4096]{2,1,0:T(8,128)(2,1)}, bf16[1,768,4096]{2,1,0:T(8,128)(2,1)S(1)}, u32[]{:S(2)}, u32[]{:S(2)}) %collective-permute-start) | collective-permute-done | bytes 6291488 | tf_op jit(solution)/shard_map/ppermute | solution.py:18
  297.3 2.6 copy-done
  299.9 120.0 %collective-permute-start.1 = (bf16[1,768,4096]{2,1,0:T(8,128)(2,1)S(1)}, bf16[1,768,4096]{2,1,0:T(8,128)(2,1)}, u32[]{:S(2)}, u32[]{:S(2)}) collective-permute-start(bf16[1,768,4096]{2,1,0:T(8,128)(2,1)S(1)} %collective-permute-done), channel_id=1, source_target_pairs={{0,1},{1,2},{2,3},{3,0},{4,5},{5,6},{6,7},{7,4},{8,9},{9,10},{10,1... | collective-permute-start | bytes 18874376 | tf_op jit(solution)/shard_map/ppermute | solution.py:18
  419.9 260.2 %collective-permute-done.1 = bf16[1,768,4096]{2,1,0:T(8,128)(2,1)} collective-permute-done((bf16[1,768,4096]{2,1,0:T(8,128)(2,1)S(1)}, bf16[1,768,4096]{2,1,0:T(8,128)(2,1)}, u32[]{:S(2)}, u32[]{:S(2)}) %collective-permute-start.1) | collective-permute-done | bytes 6291488 | tf_op jit(solution)/shard_map/ppermute | solution.py:18
  680.1 47.7 %collective-permute-start.2 = (bf16[1,768,4096]{2,1,0:T(8,128)(2,1)}, bf16[1,768,4096]{2,1,0:T(8,128)(2,1)}, u32[]{:S(2)}, u32[]{:S(2)}) collective-permute-start(bf16[1,768,4096]{2,1,0:T(8,128)(2,1)} %collective-permute-done.1), channel_id=1, source_target_pairs={{0,1},{1,2},{2,3},{3,0},{4,5},{5,6},{6,7},{7,4},{8,9},{9,10},{10,1... | collective-permute-start | bytes 18874376 | tf_op jit(solution)/shard_map/ppermute | solution.py:18
  727.9 2.0 reshape.157
  729.9 3.3 reshape.161
  733.2 249.9 %collective-permute-done.2 = bf16[1,768,4096]{2,1,0:T(8,128)(2,1)} collective-permute-done((bf16[1,768,4096]{2,1,0:T(8,128)(2,1)}, bf16[1,768,4096]{2,1,0:T(8,128)(2,1)}, u32[]{:S(2)}, u32[]{:S(2)}) %collective-permute-start.2) | collective-permute-done | bytes 6291488 | tf_op jit(solution)/shard_map/ppermute | solution.py:18
  983.1 20.8 %pad_maximum_fusion = bf16[4,1,768,4096]{3,2,1,0:T(8,128)(2,1)} fusion(bf16[1,1,768,4096]{3,2,1,0:T(8,128)(2,1)} %bitcast.6, bf16[1,1,768,4096]{3,2,1,0:T(8,128)(2,1)} %bitcast.5, bf16[1,1,768,4096]{3,2,1,0:T(8,128)(2,1)} %bitcast.75, bf16[1,1,768,4096]{3,2,1,0:T(8,128)(2,1)} %bitcast.74), kind=kLoop, calls=%fused_computation.4 | loop fusion | flops 37748736 | bytes 50331648 | tf_op jit(solution)/shard_map/stack | solution.py:20
  1003.9 19.1 %slice_bitcast_fusion.3 = (bf16[4,768,1024]{2,1,0:T(8,128)(2,1)}, bf16[4,768,1024]{2,1,0:T(8,128)(2,1)}, bf16[4,768,1024]{2,1,0:T(8,128)(2,1)}, bf16[4,768,1024]{2,1,0:T(8,128)(2,1)}) fusion(bf16[4,1,768,4096]{3,2,1,0:T(8,128)(2,1)} %pad_maximum_fusion), kind=kLoop, calls=%fused_computation.17 | loop fusion | bytes 50331648 | tf_op jit(solution)/shard_map/gather | solution.py:20
  1023.0 6.4 gather_fusion.1
  1029.4 6.4 gather_fusion.2
  1035.8 6.4 gather_fusion.3
  1042.2 6.3 gather_fusion
  1048.5 17.7 %pad_maximum_fusion.1 = bf16[4,1,768,4096]{3,2,0,1:T(8,128)(2,1)} fusion(bf16[4,1,768,1024]{3,2,0,1:T(8,128)(2,1)} %bitcast.72, bf16[4,1,768,1024]{3,2,0,1:T(8,128)(2,1)} %bitcast.71, bf16[4,1,768,1024]{3,2,0,1:T(8,128)(2,1)} %bitcast.70, bf16[4,1,768,1024]{3,2,0,1:T(8,128)(2,1)} %bitcast.73), kind=kLoop, calls=%fused_computation.5 | loop fusion | flops 100663296 | bytes 50331648
  1066.2 14.4 %fusion.39 = f32[292,4096]{1,0:T(8,128)} fusion(bf16[292,3072]{1,0:T(8,128)(2,1)S(1)} %reshape.157, bf16[3072,4096]{1,0:T(8,128)(2,1)} %bitcast.68), kind=kOutput, calls=%fused_computation.62 | convolution fusion | flops 7348420608 | bytes 31744000 | tf_op jit(solution)/shard_map/dot_general | solution.py:71
  1080.6 14.5 %fusion.6 = f32[292,4096]{1,0:T(8,128)} fusion(bf16[292,3072]{1,0:T(8,128)(2,1)S(1)} %reshape.157, bf16[1,3072,4096]{2,1,0:T(8,128)(2,1)} %all-gather.7.cloned.1.call-done), kind=kOutput, calls=%fused_computation.12 | convolution fusion | flops 7348420608 | bytes 31744000 | tf_op jit(solution)/shard_map/dot_general | solution.py:72
  1095.1 172.6 %all-gather.9.cloned.1.call-done = bf16[1,4096,3072]{2,1,0:T(8,128)(2,1)} async-done(((bf16[1,4096,768]{2,1,0:T(8,128)(2,1)}), bf16[1,4096,3072]{2,1,0:T(8,128)(2,1)}) %all-gather.9.cloned.1.call-update) | async-done | bytes 25165840 | tf_op jit(solution)/shard_map/all_gather | solution.py:74
  1267.8 14.5 %fusion = f32[292,4096]{1,0:T(8,128)} fusion(bf16[292,3072]{1,0:T(8,128)(2,1)} %reshape.161, bf16[1,4096,3072]{2,1,0:T(8,128)(2,1)} %all-gather.9.cloned.1.call-done), kind=kOutput, calls=%fused_computation.6 | convolution fusion | flops 7348420608 | bytes 31744000 | tf_op jit(solution)/shard_map/dot_general | solution.py:86
  1282.3 21.1 %fusion.18 = f32[292,3072]{1,0:T(8,128)} fusion(bf16[3072,4096]{1,0:T(8,128)(2,1)} %bitcast.69, f32[292,4096]{1,0:T(8,128)} %fusion.39, f32[292,4096]{1,0:T(8,128)} %fusion, f32[292,4096]{1,0:T(8,128)} %fusion.6), kind=kOutput, calls=%fused_computation.28 | convolution fusion | flops 7360380928 | bytes 43106304 | tf_op jit(solution)/shard_map/dot_general | solution.py:94
  1303.4 17.0 %fusion.12 = bf16[292,3072]{1,0:T(8,128)(2,1)} fusion(f32[292,3072]{1,0:T(8,128)} %fusion.18, bf16[1,3072,4096]{2,1,0:T(8,128)(2,1)} %all-gather.7.cloned.1.call-done, f32[292,4096]{1,0:T(8,128)} %fusion, f32[292,4096]{1,0:T(8,128)} %fusion.39), kind=kOutput, calls=%fused_computation.24 | convolution fusion | flops 7357390848 | bytes 40116224 | tf_op jit(solution)/shard_map/dot_general | solution.py:95
  1320.4 17.2 %fusion.15 = bf16[292,3072]{1,0:T(8,128)(2,1)} fusion(bf16[1,4096,3072]{2,1,0:T(8,128)(2,1)} %all-gather.9.cloned.1.call-done, f32[292,4096]{1,0:T(8,128)} %fusion.6, f32[292,4096]{1,0:T(8,128)} %fusion.39), kind=kOutput, calls=%fused_computation.25 | convolution fusion | flops 7356493824 | bytes 36528128 | tf_op jit(solution)/shard_map/dot_general | solution.py:75
  1337.7 2.4 reshape.162
  1340.2 3.5 all-to-all-start.3
  1344.3 2.4 reshape.158
  1346.7 10.4 all-to-all-done.3
  1357.1 3.5 all-to-all-start.1
  1363.4 9.7 all-to-all-done.1
  1373.4 2.7 multiply_reduce_fusion
  1376.1 3.0 psum.7
  (65 shorter events, 15.2 us)
Async XLA Ops:
  7.2 24.7 %copy-start.1 = (bf16[128,1536]{1,0:T(8,128)(2,1)S(1)}, bf16[128,1536]{1,0:T(8,128)(2,1)}, u32[]{:S(2)}) copy-start(bf16[128,1536]{1,0:T(8,128)(2,1)} %param.10) | copy-start | bytes 1179652
  7.2 720.7 %all-gather.5.cloned.1.call-start = ((), (), s32[]{:S(2)}) async-start(), calls=%async_computation.6 | async-start | bytes 2949120 | tf_op jit(solution)/shard_map/all_gather | solution.py:64
  10.0 0.6 copy-start.3
  12.8 20.5 %copy-start.6 = (f32[128,2]{0,1:T(2,128)S(1)}, f32[128,2]{0,1:T(2,128)}, u32[]{:S(2)}) copy-start(f32[128,2]{0,1:T(2,128)} %param.9) | copy-start | bytes 3076
  31.8 698.2 %all-gather.11.cloned.1.call-start = ((), (), s32[]{:S(2)}) async-start(), calls=%async_computation.10 | async-start | bytes 2949120 | tf_op jit(solution)/shard_map/all_gather | solution.py:83
  50.1 1030.6 %all-gather.7.cloned.1.call-start = ((), (), s32[]{:S(2)}) async-start(), calls=%async_computation.7 | async-start | bytes 31457280 | tf_op jit(solution)/shard_map/all_gather | solution.py:69
  50.8 1216.9 %all-gather.9.cloned.1.call-start = ((), (), s32[]{:S(2)}) async-start(), calls=%async_computation.8 | async-start | bytes 31457280 | tf_op jit(solution)/shard_map/all_gather | solution.py:74
  51.4 1286.3 %reduce-scatter.5.cloned.1.call-start = ((), (), s32[]{:S(2)}) async-start(), calls=%async_computation.11 | async-start | bytes 2727936 | tf_op jit(solution)/shard_map/reduce_scatter | solution.py:98
  51.4 245.9 %collective-permute-start = (bf16[1,768,4096]{2,1,0:T(8,128)(2,1)}, bf16[1,768,4096]{2,1,0:T(8,128)(2,1)S(1)}, u32[]{:S(2)}, u32[]{:S(2)}) collective-permute-start(bf16[1,768,4096]{2,1,0:T(8,128)(2,1)} %param.11), channel_id=1, source_target_pairs={{0,1},{1,2},{2,3},{3,0},{4,5},{5,6},{6,7},{7,4},{8,9},{9,10},{10,1... | collective-permute-start | bytes 18874376 | tf_op jit(solution)/shard_map/ppermute | solution.py:18
  297.3 2.6 copy-start
  299.9 380.2 %collective-permute-start.1 = (bf16[1,768,4096]{2,1,0:T(8,128)(2,1)S(1)}, bf16[1,768,4096]{2,1,0:T(8,128)(2,1)}, u32[]{:S(2)}, u32[]{:S(2)}) collective-permute-start(bf16[1,768,4096]{2,1,0:T(8,128)(2,1)S(1)} %collective-permute-done), channel_id=1, source_target_pairs={{0,1},{1,2},{2,3},{3,0},{4,5},{5,6},{6,7},{7,4},{8,9},{9,10},{10,1... | collective-permute-start | bytes 18874376 | tf_op jit(solution)/shard_map/ppermute | solution.py:18
  680.1 303.1 %collective-permute-start.2 = (bf16[1,768,4096]{2,1,0:T(8,128)(2,1)}, bf16[1,768,4096]{2,1,0:T(8,128)(2,1)}, u32[]{:S(2)}, u32[]{:S(2)}) collective-permute-start(bf16[1,768,4096]{2,1,0:T(8,128)(2,1)} %collective-permute-done.1), channel_id=1, source_target_pairs={{0,1},{1,2},{2,3},{3,0},{4,5},{5,6},{6,7},{7,4},{8,9},{9,10},{10,1... | collective-permute-start | bytes 18874376 | tf_op jit(solution)/shard_map/ppermute | solution.py:18
  1320.4 23.9 %reduce-scatter.3.cloned.1.call-start = ((), (), s32[]{:S(2)}) async-start(), calls=%async_computation.9 | async-start | bytes 2727936 | tf_op jit(solution)/shard_map/reduce_scatter | solution.py:76
  1337.7 22.9 %copy-start.4 = (s32[256]{0:T(256)S(1)}, s32[256]{0:T(256)}, u32[]{:S(2)}) copy-start(s32[256]{0:T(256)} %copy-done.3) | copy-start | bytes 3076
  1337.7 23.1 %copy-start.2 = (bf16[128,1536]{1,0:T(8,128)(2,1)S(1)}, bf16[128,1536]{1,0:T(8,128)(2,1)}, u32[]{:S(2)}) copy-start(bf16[128,1536]{1,0:T(8,128)(2,1)} %param.10) | copy-start | bytes 1179652
  1337.7 24.1 %copy-start.5 = (s32[128,2]{0,1:T(2,128)S(1)}, s32[128,2]{0,1:T(2,128)}, u32[]{:S(2)}) copy-start(s32[128,2]{0,1:T(2,128)} %param.8) | copy-start | bytes 3076
  1340.2 16.9 %all-to-all-start.3 = ((bf16[4,73,1536]{2,1,0:T(8,128)(2,1)}), bf16[4,73,1536]{2,1,0:T(8,128)(2,1)S(1)}, u32[]{:S(2)}, u32[]{:S(2)}) async-start(bf16[4,73,1536]{2,1,0:T(8,128)(2,1)} %reshape.162), calls=%async_computation.5 | async-start | bytes 1966080 | tf_op jit(solution)/shard_map/all_to_all | solution.py:101
  1343.7 29.7 %copy-start.7 = (f32[128,2]{0,1:T(2,128)S(1)}, f32[128,2]{0,1:T(2,128)}, u32[]{:S(2)}) copy-start(f32[128,2]{0,1:T(2,128)} %param.9) | copy-start | bytes 3076
  1357.1 16.1 %all-to-all-start.1 = ((bf16[4,73,1536]{2,1,0:T(8,128)(2,1)}), bf16[4,73,1536]{2,1,0:T(8,128)(2,1)S(1)}, u32[]{:S(2)}, u32[]{:S(2)}) async-start(bf16[4,73,1536]{2,1,0:T(8,128)(2,1)} %reshape.158), calls=%async_computation.2 | async-start | bytes 1966080 | tf_op jit(solution)/shard_map/all_to_all | solution.py:79
Sparse Core Ops, SparseCore 0:
  31.9 9.9 all-gather.4
  50.2 9.9 all-gather.10
  61.7 667.5 all-gather.6
  730.8 536.9 all-gather.8
  1320.5 6.7 reduce-scatter.4
  1337.8 6.4 reduce-scatter.2
